TPU v7x, 128 devices: a whole 4x4x4 slice. The times are simulated.
128 devices in a mesh: dp: 16 (over y, x), expert: 4 (over z), tensor: 2 (over core).
Axes of the slice: x: 4, y: 4, z: 4, core: 2. Of those that a mesh axis runs over, the one named last changes fastest.
Arguments:
- tokens: bfloat16 [8192, 2048], P(('dp', 'expert')), may hold values from -6 to 6
- expert_ids: int32 [8192, 2], P(('dp', 'expert')), may hold values from 0 to 3, all different within a row; in each aligned block of 128 rows (0 to 127, 128 to 255, ...) at most 96 rows name the same one
- gate_values: float32 [8192, 2], P(('dp', 'expert')), may hold values from 0.1 to 1
- tag_labels: int32 [8192], P(('dp', 'expert')), may hold values from 0 to 31
- w_gate: bfloat16 [4, 2048, 7168], P('expert', 'dp', 'tensor'), may hold values from -0.125 to 0.125
- w_up: bfloat16 [4, 2048, 7168], P('expert', 'dp', 'tensor'), may hold values from -0.125 to 0.125
- w_down: bfloat16 [4, 7168, 2048], P('expert', 'tensor', 'dp'), may hold values from -0.0625 to 0.0625
- adapter_in: bfloat16 [4, 16, 2048], P('expert'), may hold values from -0.125 to 0.125
- adapter_out: bfloat16 [4, 16, 7168], P('expert', None, 'tensor'), may hold values from -1.5 to 1.5
- tag_weight: bfloat16 [2048, 32], replicated, may hold values from -0.125 to 0.125
Outputs:
- layer_out: bfloat16 [8192, 2048], P(('dp', 'expert'), 'tensor')
- in_gradient: float32 [4, 16, 2048], P('expert')
- out_gradient: float32 [4, 16, 7168], P('expert', None, 'tensor')
Inputs may be any that keep to these rules, and one draw needn't show every extreme that they name: `expert_ids`: each row names 2 different experts; the rows of one index of dp and expert name each expert at most 96 times, a bound that some block reaches.
All inputs are finite; a program needn't handle non-finite values.
Results may differ from a plain program's by a relative error of at most 0.017.
Values may be sent and summed in bfloat16 or wider, within the bound.
A program may use at most 128 MiB of HBM per device.

v0:
```python
import jax
import jax.numpy as jnp
from jax import lax
from jax.sharding import PartitionSpec as P

adapter_scale = 2.0


def contract_last(left, right):
    return lax.dot_general(
        left, right, (((1,), (1,)), ((), ())), preferred_element_type=jnp.float32
    )


def contract_first(left, right):
    return lax.dot_general(
        left, right, (((0,), (0,)), ((), ())), preferred_element_type=jnp.float32
    )


def tag_gradient(logits, tag_labels):
    exp_logits = jnp.exp(logits)
    probability = exp_logits / jnp.sum(exp_logits, axis=1, keepdims=True)
    labels_hot = (
        tag_labels[:, None] == jnp.arange(logits.shape[1], dtype=jnp.int32)[None, :]
    ).astype(jnp.float32)
    return probability - labels_hot


def local(
    tokens,
    expert_ids,
    gate_values,
    tag_labels,
    w_gate,
    w_up,
    w_down,
    adapter_in,
    adapter_out,
    tag_weight,
):
    experts = lax.axis_size("expert")
    shards = lax.axis_size("tensor")
    tok_count = tokens.shape[0]
    model_width = tokens.shape[1]
    share_width = model_width // shards
    capacity = 3 * tok_count // experts
    slot_count = experts * capacity
    flat_ids = expert_ids.reshape(-1)
    onehot = (flat_ids[:, None] == jnp.arange(experts, dtype=jnp.int32)[None, :]).astype(jnp.int32)
    before = jnp.cumsum(onehot, axis=0) - onehot
    position = jnp.sum(before * onehot, axis=1)
    slot_index = (flat_ids * capacity + position).reshape(tok_count, expert_ids.shape[1])
    matches = jnp.arange(slot_count, dtype=jnp.int32)[:, None, None] == slot_index[None, :, :]
    dispatch = jnp.sum(matches.astype(jnp.float32), axis=2).astype(jnp.bfloat16)
    combine = jnp.sum(jnp.where(matches, gate_values[None, :, :], jnp.float32(0.0)), axis=2).T
    outgoing = jnp.dot(dispatch, tokens, preferred_element_type=jnp.float32).astype(jnp.bfloat16)
    arrived = lax.all_to_all(
        outgoing.reshape(experts, capacity, model_width),
        "expert",
        split_axis=0,
        concat_axis=0,
        tiled=True,
    ).reshape(slot_count, model_width)
    gate_acc = jnp.dot(
        arrived,
        lax.all_gather(w_gate, "dp", axis=1, tiled=True)[0],
        preferred_element_type=jnp.float32,
    )
    up_acc = jnp.dot(
        arrived,
        lax.all_gather(w_up, "dp", axis=1, tiled=True)[0],
        preferred_element_type=jnp.float32,
    )
    low_rank = contract_last(arrived, adapter_in[0]).astype(jnp.bfloat16)
    up_full = up_acc + adapter_scale * jnp.dot(
        low_rank, adapter_out[0], preferred_element_type=jnp.float32
    )
    activated = jax.nn.silu(gate_acc)
    hidden = (activated * up_full).astype(jnp.bfloat16)
    down_full = lax.all_gather(w_down, "dp", axis=2, tiled=True)[0]
    partial_value = jnp.dot(hidden, down_full, preferred_element_type=jnp.float32)
    column_start = lax.axis_index("tensor") * share_width
    summed = lax.psum(partial_value, "tensor").astype(jnp.bfloat16)
    returned = lax.all_to_all(
        summed.reshape(experts, capacity, model_width),
        "expert",
        split_axis=0,
        concat_axis=0,
        tiled=True,
    ).reshape(slot_count, model_width)
    mixed_rows = tokens.astype(jnp.float32) + jnp.dot(
        combine, returned.astype(jnp.float32), precision=lax.Precision.HIGHEST
    )
    layer_full = mixed_rows.astype(jnp.bfloat16)
    logits = jnp.dot(layer_full, tag_weight, preferred_element_type=jnp.float32)
    logit_grad = tag_gradient(logits, tag_labels)
    upstream = jnp.dot(
        logit_grad, tag_weight.astype(jnp.float32).T, precision=lax.Precision.HIGHEST
    )
    slot_out = jnp.dot(combine.T, upstream, precision=lax.Precision.HIGHEST).astype(jnp.bfloat16)
    slot_grad = lax.all_to_all(
        slot_out.reshape(experts, capacity, model_width),
        "expert",
        split_axis=0,
        concat_axis=0,
        tiled=True,
    ).reshape(slot_count, model_width)
    layer_out = lax.dynamic_slice_in_dim(layer_full, column_start, share_width, 1)
    hidden_grad = contract_last(slot_grad, down_full)
    up_grad = (hidden_grad * activated).astype(jnp.bfloat16)
    out_local = adapter_scale * contract_first(low_rank, up_grad)
    low_grad = adapter_scale * contract_last(up_grad, adapter_out[0])
    in_local = lax.dot_general(
        low_grad,
        arrived.astype(jnp.float32),
        (((0,), (0,)), ((), ())),
        precision=lax.Precision.HIGHEST,
    )
    in_total = lax.psum(in_local.astype(jnp.bfloat16), ("dp", "tensor")).astype(jnp.float32)
    out_total = lax.psum(out_local.astype(jnp.bfloat16), "dp").astype(jnp.float32)
    return (layer_out, in_total[None], out_total[None])


def solution(mesh):
    in_specs = (
        P(("dp", "expert"), None),
        P(("dp", "expert"), None),
        P(("dp", "expert"), None),
        P(("dp", "expert")),
        P("expert", "dp", "tensor"),
        P("expert", "dp", "tensor"),
        P("expert", "tensor", "dp"),
        P("expert", None, None),
        P("expert", None, "tensor"),
        P(),
    )
    out_specs = (
        P(("dp", "expert"), "tensor"),
        P("expert", None, None),
        P("expert", None, "tensor"),
    )
    return jax.shard_map(local, mesh=mesh, in_specs=in_specs, out_specs=out_specs, check_vma=False)
```

profile of v0, /device:TPU:0, one launch (start us, length us, event | category | flops | bytes accessed | tf_op | source)
XLA Modules:
  0.0 610.8 jit_solution(16985919612496595279)
XLA Ops:
  7.2 0.0 all-gather.6.cloned.1.call-start
  7.2 0.7 all-gather.6.cloned.1.call-update
  7.9 0.0 all-gather.4.cloned.1.call-start
  8.0 0.7 all-gather.4.cloned.1.call-update
  8.7 0.0 all-gather.8.cloned.1.call-start
  8.7 0.7 all-gather.8.cloned.1.call-update
  9.4 0.8 copy.31
  10.2 0.1 eq.56
  10.4 0.1 eq.52
  10.5 1.2 reduce-window.6
  11.8 0.1 slice.8
  11.8 0.1 copy.33
  12.0 0.1 copy.34
  12.1 0.1 add_bitcast_fusion
  12.2 0.1 reduce_sum.39
  12.3 0.1 copy.35
  12.4 0.7 multiply_add_fusion
  13.1 0.8 convert_reduce_fusion
  13.9 0.6 convolution_convert_fusion.1
  14.4 25.9 %all_to_all.15 = bf16[4,96,2048]{2,1,0:T(8,128)(2,1)S(1)} all-to-all(bf16[4,96,2048]{2,1,0:T(8,128)(2,1)S(1)} %bitcast.78), channel_id=1, replica_groups=mesh['dp'=16,'expert'=4,'tensor'=2] {'expert'}, dimensions={0} | all-to-all | bytes 3145728 | tf_op jit(solution)/shard_map/all_to_all | solution.py:58
  40.4 0.5 convolution_convert_fusion.3
  40.9 72.1 %all-gather.6.cloned.1.call-done = bf16[1,2048,3584]{2,1,0:T(8,128)(2,1)} async-done(((bf16[1,128,3584]{2,1,0:T(8,128)(2,1)}), bf16[1,2048,3584]{2,1,0:T(8,128)(2,1)}) %all-gather.6.cloned.1.call-update) | async-done | bytes 14680080 | tf_op jit(solution)/shard_map/all_gather | solution.py:72
  113.0 11.5 %fusion.4 = f32[384,3584]{1,0:T(8,128)} fusion(bf16[384,2048]{1,0:T(8,128)(2,1)S(1)} %bitcast.75, bf16[1,2048,3584]{2,1,0:T(8,128)(2,1)} %all-gather.6.cloned.1.call-done), kind=kOutput, calls=%fused_computation.4 | convolution fusion | flops 5637144576 | bytes 21757952 | tf_op jit(solution)/shard_map/dot_general | solution.py:70
  124.5 90.7 %all-gather.4.cloned.1.call-done = bf16[1,2048,3584]{2,1,0:T(8,128)(2,1)} async-done(((bf16[1,128,3584]{2,1,0:T(8,128)(2,1)}), bf16[1,2048,3584]{2,1,0:T(8,128)(2,1)}) %all-gather.4.cloned.1.call-update) | async-done | bytes 14680080 | tf_op jit(solution)/shard_map/all_gather | solution.py:67
  215.2 11.1 %divide_multiply_fusion = f32[384,3584]{1,0:T(8,128)} fusion(bf16[384,2048]{1,0:T(8,128)(2,1)S(1)} %bitcast.76, bf16[1,2048,3584]{2,1,0:T(8,128)(2,1)} %all-gather.4.cloned.1.call-done), kind=kOutput, calls=%fused_computation.14 | convolution fusion | flops 5642649600 | bytes 21757952 | tf_op jit(solution)/shard_map/dot_general | solution.py:65
  226.4 99.8 %all-gather.8.cloned.1.call-done = bf16[1,3584,2048]{2,1,0:T(8,128)(2,1)} async-done(((bf16[1,3584,128]{2,1,0:T(8,128)(2,1)}), bf16[1,3584,2048]{2,1,0:T(8,128)(2,1)}) %all-gather.8.cloned.1.call-update) | async-done | bytes 14680080 | tf_op jit(solution)/shard_map/all_gather | solution.py:81
  326.1 15.2 %fusion.2 = f32[384,2048]{1,0:T(8,128)} fusion(bf16[1,3584,2048]{2,1,0:T(8,128)(2,1)} %all-gather.8.cloned.1.call-done, f32[384,3584]{1,0:T(8,128)} %divide_multiply_fusion, f32[384,3584]{1,0:T(8,128)} %fusion.4, bf16[384,16]{0,1:T(8,128)(2,1)S(1)} %convolution_convert_fusion.3, bf16[1,16,3584]{2,1,0:T(8,128)(2,1)S(1)} %copy-done.4), kind=kOutput, calls=%fused_computation.2 | convolution fusion | flops 5686689792 | bytes 28962816 | tf_op jit(solution)/shard_map/dot_general | solution.py:82
  341.3 12.2 %all-reduce.7 = bf16[384,2048]{1,0:T(8,128)(2,1)S(1)} all-reduce(f32[384,2048]{1,0:T(8,128)} %fusion.2), channel_id=1, replica_groups=mesh['dp'=16,'expert'=4,'tensor'=2] {'tensor'}, use_global_device_ids=true, to_apply=%region_5.6 | all-reduce | flops 786432 | bytes 4718592 | tf_op jit(solution)/shard_map/psum | solution.py:84
  353.6 25.5 %all_to_all.16 = bf16[4,96,2048]{2,1,0:T(8,128)(2,1)S(1)} all-to-all(bf16[4,96,2048]{2,1,0:T(8,128)(2,1)S(1)} %bitcast.80), channel_id=1, replica_groups=mesh['dp'=16,'expert'=4,'tensor'=2] {'expert'}, dimensions={0} | all-to-all | bytes 3145728 | tf_op jit(solution)/shard_map/all_to_all | solution.py:85
  379.0 1.0 fusion.21
  380.1 0.3 fusion.38
  380.4 0.6 fusion.28
  381.0 3.7 convolution_convert_fusion
  384.8 4.4 all-to-all-start.2
  389.1 0.0 all-reduce.4.cloned.1.call-start
  389.2 20.4 %all-to-all-done.2 = bf16[4,96,2048]{2,1,0:T(8,128)(2,1)} async-done(((bf16[4,96,2048]{2,1,0:T(8,128)(2,1)}), bf16[4,96,2048]{2,1,0:T(8,128)(2,1)}, u32[]{:S(2)}, u32[]{:S(2)}) %all-to-all-start.2) | async-done | bytes 1572896 | tf_op jit(solution)/shard_map/all_to_all | solution.py:102
  409.6 10.4 %fusion.13 = bf16[384,3584]{1,0:T(8,128)(2,1)S(1)} fusion(f32[384,3584]{1,0:T(8,128)} %divide_multiply_fusion, bf16[384,2048]{1,0:T(8,128)(2,1)} %bitcast.12, bf16[1,3584,2048]{2,1,0:T(8,128)(2,1)} %all-gather.8.cloned.1.call-done), kind=kOutput, calls=%fused_computation.12 | convolution fusion | flops 5639897088 | bytes 24510464 | tf_op jit(solution)/shard_map/dot_general | solution.py:10
  420.0 0.8 convolution_multiply_fusion.2
  420.9 0.6 copy-done.2
  421.4 1.4 fusion.22
  422.8 0.0 all-reduce.4.cloned.1.call-update
  422.8 0.0 all-reduce.6.cloned.1.call-start
  422.9 1.1 fusion.20
  424.0 0.7 constant_dynamic-slice_fusion
  424.7 92.3 %all-reduce.4.cloned.1.call-done = bf16[1,16,2048]{2,1,0:T(8,128)(2,1)} async-done(((bf16[1,16,2048]{2,1,0:T(8,128)(2,1)}), bf16[1,16,2048]{2,1,0:T(8,128)(2,1)}) %all-reduce.4.cloned.1.call-update) | async-done | bytes 65552 | tf_op jit(solution)/shard_map/psum | solution.py:120
  517.0 1.5 broadcast_in_dim.33
  518.5 84.1 %all-reduce.6.cloned.1.call-done = bf16[1,16,3584]{2,1,0:T(8,128)(2,1)} async-done(((bf16[1,16,3584]{2,1,0:T(8,128)(2,1)}), bf16[1,16,3584]{2,1,0:T(8,128)(2,1)}) %all-reduce.6.cloned.1.call-update) | async-done | bytes 114704 | tf_op jit(solution)/shard_map/psum | solution.py:121
  602.7 1.6 broadcast_in_dim.35
  (18 shorter events, 0.1 us)
Async XLA Ops:
  7.2 372.9 %copy-start = (bf16[2048,32]{0,1:T(8,128)(2,1)S(1)}, bf16[2048,32]{0,1:T(8,128)(2,1)}, u32[]{:S(2)}) copy-start(bf16[2048,32]{0,1:T(8,128)(2,1)} %param.19) | copy-start | bytes 393220
  7.2 6.7 %copy-start.3 = (bf16[128,2048]{1,0:T(8,128)(2,1)S(1)}, bf16[128,2048]{1,0:T(8,128)(2,1)}, u32[]{:S(2)}) copy-start(bf16[128,2048]{1,0:T(8,128)(2,1)} %param.10) | copy-start | bytes 1572868
  7.2 105.8 %all-gather.6.cloned.1.call-start = ((), (), s32[]{:S(2)}) async-start(), calls=%async_computation.4 | async-start | bytes 15597568 | tf_op jit(solution)/shard_map/all_gather | solution.py:72
  7.9 207.3 %all-gather.4.cloned.1.call-start = ((), (), s32[]{:S(2)}) async-start(), calls=%async_computation.3 | async-start | bytes 15597568 | tf_op jit(solution)/shard_map/all_gather | solution.py:67
  8.7 317.4 %all-gather.8.cloned.1.call-start = ((), (), s32[]{:S(2)}) async-start(), calls=%async_computation.5 | async-start | bytes 15597568 | tf_op jit(solution)/shard_map/all_gather | solution.py:81
  9.4 31.0 %copy-start.5 = (bf16[1,16,2048]{2,1,0:T(8,128)(2,1)S(1)}, bf16[1,16,2048]{2,1,0:T(8,128)(2,1)}, u32[]{:S(2)}) copy-start(bf16[1,16,2048]{2,1,0:T(8,128)(2,1)} %param.17) | copy-start | bytes 196612
  40.4 174.9 %copy-start.1 = (bf16[4,96,2048]{2,1,0:T(8,128)(2,1)}, bf16[4,96,2048]{2,1,0:T(8,128)(2,1)S(1)}, u32[]{:S(2)}) copy-start(bf16[4,96,2048]{2,1,0:T(8,128)(2,1)S(1)} %all_to_all.15) | copy-start | bytes 4718596
  124.5 201.6 %copy-start.4 = (bf16[1,16,3584]{2,1,0:T(8,128)(2,1)S(1)}, bf16[1,16,3584]{2,1,0:T(8,128)(2,1)}, u32[]{:S(2)}) copy-start(bf16[1,16,3584]{2,1,0:T(8,128)(2,1)} %param.18) | copy-start | bytes 344068
  353.6 26.8 %copy-start.6 = (s32[128]{0:T(128)S(1)}, s32[128]{0:T(128)}, u32[]{:S(2)}) copy-start(s32[128]{0:T(128)} %param.13) | copy-start | bytes 1540
  384.8 24.8 %all-to-all-start.2 = ((bf16[4,96,2048]{2,1,0:T(8,128)(2,1)}), bf16[4,96,2048]{2,1,0:T(8,128)(2,1)}, u32[]{:S(2)}, u32[]{:S(2)}) async-start(bf16[4,96,2048]{2,1,0:T(8,128)(2,1)} %bitcast.11), calls=%async_computation.2 | async-start | bytes 3145728 | tf_op jit(solution)/shard_map/all_to_all | solution.py:102
  389.1 127.9 %all-reduce.4.cloned.1.call-start = ((), (), s32[]{:S(2)}) async-start(), calls=%async_computation.6 | async-start | bytes 131072 | tf_op jit(solution)/shard_map/psum | solution.py:120
  420.0 1.4 copy-start.2
  422.8 179.9 %all-reduce.6.cloned.1.call-start = ((), (), s32[]{:S(2)}) async-start(), calls=%async_computation.7 | async-start | bytes 229376 | tf_op jit(solution)/shard_map/psum | solution.py:121
Sparse Core Ops, SparseCore 0:
  10.1 102.8 all-gather.5
  115.2 100.0 all-gather.3
  217.4 108.6 all-gather.7
  422.9 94.0 all-reduce.3
  520.7 81.9 all-reduce.5
where the time goes:
time: 611 us
  waiting for transfers between devices  462 us (76%)
  blocking collectives  63.6 us (10%)
  matrix products  58.3 us (10%)
  between operations  13.9 us (2%)
    all_gather x1, waiting for transfers between devices, local(): down_full = lax.all_gather(w_down, 'dp', axis=2, tiled=True)[0]  99.8 us
    psum x1, waiting for transfers between devices, local(): lax.psum(in_local.astype(jnp.bfloat16), ('dp', 'tensor'))  92.3 us
    all_gather x1, waiting for transfers between devices, local(): lax.all_gather(w_gate, 'dp', axis=1, tiled=True)[0]  90.7 us
    psum x1, waiting for transfers between devices, local(): lax.psum(out_local.astype(jnp.bfloat16), 'dp').astype(jnp.float32)  84.1 us
    all_gather x1, waiting for transfers between devices, local(): lax.all_gather(w_up, 'dp', axis=1, tiled=True)[0]  72.1 us
    all_to_all x1, blocking collectives, local(): lax.all_to_all(outgoing.reshape(experts, capacity, model_width), 'expert'...  25.9 us
    all_to_all x1, blocking collectives, local(): lax.all_to_all(summed.reshape(experts, capacity, model_width), 'expert',...  25.5 us
    all_to_all x1, waiting for transfers between devices, local(): lax.all_to_all(slot_out.reshape(experts, capacity, model_width), 'expert'...  20.4 us
  transfers between devices with their start and end apart: 6, of which 6 were waited for; matrix products, arithmetic and copies ran while one was open for 5% of the time, Pallas kernels for 0%

commit v1 on v0

--- a/solution.py
+++ b/solution.py
@@ -4,6 +4,19 @@
 from jax.sharding import PartitionSpec as P
 
 adapter_scale = 2.0
+
+
+def gather_around(array, axis, dim):
+    ways = lax.axis_size(axis)
+    up = [(d, (d + 1) % ways) for d in range(ways)]
+    down = [(d, (d - 1) % ways) for d in range(ways)]
+    earlier, later = ([array], [array])
+    for _ in range(ways // 2):
+        earlier.append(lax.ppermute(earlier[-1], axis, up))
+    for _ in range((ways - 1) // 2):
+        later.append(lax.ppermute(later[-1], axis, down))
+    line = jnp.concatenate([*earlier[::-1], *later[1:]], axis=dim)
+    return jnp.roll(line, (lax.axis_index(axis) - ways // 2) * array.shape[dim], axis=dim)
 
 
 def contract_last(left, right):
@@ -78,7 +91,7 @@
     )
     activated = jax.nn.silu(gate_acc)
     hidden = (activated * up_full).astype(jnp.bfloat16)
-    down_full = lax.all_gather(w_down, "dp", axis=2, tiled=True)[0]
+    down_full = gather_around(w_down, "dp", 2)[0]
     partial_value = jnp.dot(hidden, down_full, preferred_element_type=jnp.float32)
     column_start = lax.axis_index("tensor") * share_width
     summed = lax.psum(partial_value, "tensor").astype(jnp.bfloat16)

time: 611 us -> 675 us (1.10)
  local copies, waits for them, and re-layouts: 2.94 us -> 67.5 us
  starting transfers between devices: 4.57 us -> 47 us
  blocking collectives: 63.6 us -> 37.8 us
  waiting for transfers between devices: 462 us -> 438 us
    ppermute x0 -> x15, waiting for transfers between devices: none -> 243 us  [the longest x8 228 us: gather_around(): earlier.append(lax.ppermute(earlier[-1], axis, up))]
    all_gather x1 -> x0, waiting for transfers between devices: 99.8 us -> none  [local(): down_full = lax.all_gather(w_down, 'dp', axis=2, tiled=True)[0]]
    all_gather x1, waiting for transfers between devices: 90.7 us -> 0.01 us  [local(): lax.all_gather(w_gate, 'dp', axis=1, tiled=True)[0]]
    all_gather x1, waiting for transfers between devices: 72.1 us -> 0.01 us  [local(): lax.all_gather(w_up, 'dp', axis=1, tiled=True)[0]]
    unnamed x15 -> x60, local copies, waits for them, and re-layouts: 1.42 us -> 65 us
    ppermute x0 -> x15, starting transfers between devices: none -> 38.7 us  [the longest x7 37 us: gather_around(): later.append(lax.ppermute(later[-1], axis, down))]
    all_to_all x1 -> x0, blocking collectives: 25.9 us -> none  [local(): lax.all_to_all(outgoing.reshape(experts, capacity, model_width), 'expert'...]
  transfers between devices with their start and end apart: 6 -> 21, of which waited for: 6 -> 12; matrix products, arithmetic and copies ran while one was open for 5% -> 13% of each run, Pallas kernels for 0% -> 0%
where the time goes in v1:
time: 675 us; the launch traced here: 674 us
  waiting for transfers between devices  438 us (65%)
  local copies, waits for them, and re-layouts  67.5 us (10%)
  matrix products  63 us (9%)
  starting transfers between devices  47 us (7%)
  blocking collectives  37.8 us (6%)
  between operations  14 us (2%)
    ppermute x8, waiting for transfers between devices, gather_around(): earlier.append(lax.ppermute(earlier[-1], axis, up))  228 us
    psum x1, waiting for transfers between devices, local(): lax.psum(in_local.astype(jnp.bfloat16), ('dp', 'tensor'))  89.3 us
    psum x1, waiting for transfers between devices, local(): lax.psum(out_local.astype(jnp.bfloat16), 'dp').astype(jnp.float32)  84.2 us
    unnamed x60, local copies, waits for them, and re-layouts  65 us
    ppermute x7, starting transfers between devices, gather_around(): later.append(lax.ppermute(later[-1], axis, down))  37 us
    all_to_all x1, blocking collectives, local(): lax.all_to_all(summed.reshape(experts, capacity, model_width), 'expert',...  25.5 us
    all_to_all x1, waiting for transfers between devices, local(): lax.all_to_all(slot_out.reshape(experts, capacity, model_width), 'expert'...  20.3 us
    dot_general x1, matrix products, local(): jnp.dot(hidden, down_full, preferred_element_type=jnp.float32)  15.1 us
  transfers between devices with their start and end apart: 21, of which 12 were waited for; matrix products, arithmetic and copies ran while one was open for 13% of the time, Pallas kernels for 0%

profile of v1, /device:TPU:0, one launch (start us, length us, event | category | flops | bytes accessed | tf_op | source)
XLA Modules:
  0.0 673.7 jit_solution(438240909335495655)
XLA Ops:
  10.3 30.8 %collective-permute-done = bf16[1,3584,128]{2,1,0:T(8,128)(2,1)S(1)} collective-permute-done((bf16[1,3584,128]{2,1,0:T(8,128)(2,1)}, bf16[1,3584,128]{2,1,0:T(8,128)(2,1)S(1)}, u32[]{:S(2)}, u32[]{:S(2)}) %collective-permute-start) | collective-permute-done | bytes 917536 | tf_op jit(solution)/shard_map/ppermute | solution.py:15
  41.2 5.3 collective-permute-start.8
  46.5 25.7 %collective-permute-done.1 = bf16[1,3584,128]{2,1,0:T(8,128)(2,1)} collective-permute-done((bf16[1,3584,128]{2,1,0:T(8,128)(2,1)S(1)}, bf16[1,3584,128]{2,1,0:T(8,128)(2,1)}, u32[]{:S(2)}, u32[]{:S(2)}) %collective-permute-start.1) | collective-permute-done | bytes 917536 | tf_op jit(solution)/shard_map/ppermute | solution.py:15
  72.2 5.3 collective-permute-start.9
  77.5 39.7 %collective-permute-done.2 = bf16[1,3584,128]{2,1,0:T(8,128)(2,1)S(1)} collective-permute-done((bf16[1,3584,128]{2,1,0:T(8,128)(2,1)}, bf16[1,3584,128]{2,1,0:T(8,128)(2,1)S(1)}, u32[]{:S(2)}, u32[]{:S(2)}) %collective-permute-start.2) | collective-permute-done | bytes 917536 | tf_op jit(solution)/shard_map/ppermute | solution.py:15
  118.2 5.3 collective-permute-start.10
  123.5 39.2 %collective-permute-done.3 = bf16[1,3584,128]{2,1,0:T(8,128)(2,1)S(1)} collective-permute-done((bf16[1,3584,128]{2,1,0:T(8,128)(2,1)S(1)}, bf16[1,3584,128]{2,1,0:T(8,128)(2,1)S(1)}, u32[]{:S(2)}, u32[]{:S(2)}) %collective-permute-start.3) | collective-permute-done | bytes 917536 | tf_op jit(solution)/shard_map/ppermute | solution.py:15
  163.7 4.5 collective-permute-start.11
  168.3 18.9 %collective-permute-done.4 = bf16[1,3584,128]{2,1,0:T(8,128)(2,1)} collective-permute-done((bf16[1,3584,128]{2,1,0:T(8,128)(2,1)S(1)}, bf16[1,3584,128]{2,1,0:T(8,128)(2,1)}, u32[]{:S(2)}, u32[]{:S(2)}) %collective-permute-start.4) | collective-permute-done | bytes 917536 | tf_op jit(solution)/shard_map/ppermute | solution.py:15
  190.8 5.3 collective-permute-start.12
  196.1 29.4 %collective-permute-done.5 = bf16[1,3584,128]{2,1,0:T(8,128)(2,1)} collective-permute-done((bf16[1,3584,128]{2,1,0:T(8,128)(2,1)}, bf16[1,3584,128]{2,1,0:T(8,128)(2,1)}, u32[]{:S(2)}, u32[]{:S(2)}) %collective-permute-start.5) | collective-permute-done | bytes 917536 | tf_op jit(solution)/shard_map/ppermute | solution.py:15
  227.0 2.8 convolution_convert_fusion.1
  229.8 4.5 all-to-all-start
  234.3 5.3 collective-permute-start.13
  239.6 23.5 %collective-permute-done.6 = bf16[1,3584,128]{2,1,0:T(8,128)(2,1)} collective-permute-done((bf16[1,3584,128]{2,1,0:T(8,128)(2,1)}, bf16[1,3584,128]{2,1,0:T(8,128)(2,1)}, u32[]{:S(2)}, u32[]{:S(2)}) %collective-permute-start.6) | collective-permute-done | bytes 917536 | tf_op jit(solution)/shard_map/ppermute | solution.py:15
  264.8 14.3 %collective-permute-done.13 = bf16[1,3584,128]{2,1,0:T(8,128)(2,1)} collective-permute-done((bf16[1,3584,128]{2,1,0:T(8,128)(2,1)}, bf16[1,3584,128]{2,1,0:T(8,128)(2,1)}, u32[]{:S(2)}, u32[]{:S(2)}) %collective-permute-start.13) | collective-permute-done | bytes 917536 | tf_op jit(solution)/shard_map/ppermute | solution.py:17
  279.0 5.8 collective-permute-start.14
  284.8 21.1 %collective-permute-done.7 = bf16[1,3584,128]{2,1,0:T(8,128)(2,1)} collective-permute-done((bf16[1,3584,128]{2,1,0:T(8,128)(2,1)}, bf16[1,3584,128]{2,1,0:T(8,128)(2,1)}, u32[]{:S(2)}, u32[]{:S(2)}) %collective-permute-start.7) | collective-permute-done | bytes 917536 | tf_op jit(solution)/shard_map/ppermute | solution.py:15
  308.2 2.2 constant_dynamic-update-slice_fusion.30
  310.4 2.2 constant_dynamic-update-slice_fusion.29
  312.6 2.2 constant_dynamic-update-slice_fusion.28
  314.9 2.3 constant_dynamic-update-slice_fusion.27
  322.6 2.2 constant_dynamic-update-slice_fusion.23
  324.8 2.2 constant_dynamic-update-slice_fusion.22
  327.0 2.3 constant_dynamic-update-slice_fusion.21
  331.5 2.2 constant_dynamic-update-slice_fusion.19
  333.8 2.3 constant_dynamic-update-slice_fusion.18
  336.1 2.2 constant_dynamic-update-slice_fusion.17
  339.3 2.3 constant_dynamic-update-slice_fusion.15
  341.6 2.2 constant_dynamic-update-slice_fusion.14
  343.8 2.3 constant_dynamic-update-slice_fusion.13
  346.1 2.3 constant_dynamic-update-slice_fusion.12
  350.5 2.3 constant_dynamic-update-slice_fusion.9
  360.4 2.2 constant_dynamic-update-slice_fusion.3
  362.6 2.2 constant_dynamic-update-slice_fusion.2
  364.9 2.2 constant_dynamic-update-slice_fusion.1
  368.2 11.1 %divide_multiply_fusion = f32[384,3584]{1,0:T(8,128)} fusion(bf16[384,2048]{1,0:T(8,128)(2,1)S(1)} %bitcast.75, bf16[1,2048,3584]{2,1,0:T(8,128)(2,1)} %all-gather.3.cloned.1.call-done), kind=kOutput, calls=%fused_computation.16 | convolution fusion | flops 5642649600 | bytes 21757952 | tf_op jit(solution)/shard_map/dot_general | solution.py:78
  379.3 11.5 %fusion.4 = f32[384,3584]{1,0:T(8,128)} fusion(bf16[384,2048]{1,0:T(8,128)(2,1)S(1)} %bitcast.76, bf16[1,2048,3584]{2,1,0:T(8,128)(2,1)} %all-gather.5.cloned.1.call-done), kind=kOutput, calls=%fused_computation.4 | convolution fusion | flops 5637144576 | bytes 21757952 | tf_op jit(solution)/shard_map/dot_general | solution.py:83
  390.8 15.1 %fusion.2 = f32[384,2048]{1,0:T(8,128)} fusion(bf16[1,3584,4096]{2,1,0:T(8,128)(2,1)} %constant_dynamic-update-slice_fusion, s32[]{:T(128)S(6)} %select_n.22, f32[384,3584]{1,0:T(8,128)} %divide_multiply_fusion, f32[384,3584]{1,0:T(8,128)} %fusion.4, bf16[384,16]{0,1:T(8,128)(2,1)S(1)} %convolution_convert_fusion.3, bf16[1,16,3584]{2,1,0:T(8,128)(2,1)S(1)} %copy-done.12), kind=kOutput, calls=%fused_computation.2 | convolution fusion | flops 5686689792 | bytes 28962820 | tf_op jit(solution)/shard_map/dot_general | solution.py:95
  405.9 12.2 %all-reduce.7 = bf16[384,2048]{1,0:T(8,128)(2,1)S(1)} all-reduce(f32[384,2048]{1,0:T(8,128)} %fusion.2), channel_id=1, replica_groups=mesh['dp'=16,'expert'=4,'tensor'=2] {'tensor'}, use_global_device_ids=true, to_apply=%region_5.6 | all-reduce | flops 786432 | bytes 4718592 | tf_op jit(solution)/shard_map/psum | solution.py:97
  418.2 25.5 %all_to_all.15 = bf16[4,96,2048]{2,1,0:T(8,128)(2,1)S(1)} all-to-all(bf16[4,96,2048]{2,1,0:T(8,128)(2,1)S(1)} %bitcast.79), channel_id=1, replica_groups=mesh['dp'=16,'expert'=4,'tensor'=2] {'expert'}, dimensions={0} | all-to-all | bytes 3145728 | tf_op jit(solution)/shard_map/all_to_all | solution.py:98
  445.7 3.8 convolution_convert_fusion
  449.5 3.6 all-to-all-start.2
  453.1 20.3 %all-to-all-done.2 = bf16[4,96,2048]{2,1,0:T(8,128)(2,1)S(1)} async-done(((bf16[4,96,2048]{2,1,0:T(8,128)(2,1)}), bf16[4,96,2048]{2,1,0:T(8,128)(2,1)S(1)}, u32[]{:S(2)}, u32[]{:S(2)}) %all-to-all-start.2) | async-done | bytes 1572896 | tf_op jit(solution)/shard_map/all_to_all | solution.py:115
  474.6 10.4 %fusion.15 = bf16[384,3584]{1,0:T(8,128)(2,1)S(1)} fusion(f32[384,3584]{1,0:T(8,128)} %divide_multiply_fusion, bf16[384,2048]{1,0:T(8,128)(2,1)} %bitcast.80, bf16[1,3584,4096]{2,1,0:T(8,128)(2,1)} %constant_dynamic-update-slice_fusion, s32[]{:T(128)S(6)} %select_n.22), kind=kOutput, calls=%fused_computation.14 | convolution fusion | flops 5639897088 | bytes 24510468 | tf_op jit(solution)/shard_map/dot_general | solution.py:23
  485.9 2.8 fusion.24
  490.6 89.3 %all-reduce.4.cloned.1.call-done = bf16[1,16,2048]{2,1,0:T(8,128)(2,1)} async-done(((bf16[1,16,2048]{2,1,0:T(8,128)(2,1)}), bf16[1,16,2048]{2,1,0:T(8,128)(2,1)}) %all-reduce.4.cloned.1.call-update) | async-done | bytes 65552 | tf_op jit(solution)/shard_map/psum | solution.py:133
  581.4 84.2 %all-reduce.6.cloned.1.call-done = bf16[1,16,3584]{2,1,0:T(8,128)(2,1)} async-done(((bf16[1,16,3584]{2,1,0:T(8,128)(2,1)}), bf16[1,16,3584]{2,1,0:T(8,128)(2,1)}) %all-reduce.6.cloned.1.call-update) | async-done | bytes 114704 | tf_op jit(solution)/shard_map/psum | solution.py:134
  (92 shorter events, 42.5 us)
Async XLA Ops:
  7.2 437.6 %copy-start = (bf16[2048,32]{0,1:T(8,128)(2,1)S(1)}, bf16[2048,32]{0,1:T(8,128)(2,1)}, u32[]{:S(2)}) copy-start(bf16[2048,32]{0,1:T(8,128)(2,1)} %param.19) | copy-start | bytes 393220
  7.2 346.7 %copy-start.2 = (bf16[1,3584,128]{2,1,0:T(8,128)(2,1)S(1)}, bf16[1,3584,128]{2,1,0:T(8,128)(2,1)}, u32[]{:S(2)}) copy-start(bf16[1,3584,128]{2,1,0:T(8,128)(2,1)} %param.16) | copy-start | bytes 2752516
  7.2 361.0 %all-gather.3.cloned.1.call-start = ((), (), s32[]{:S(2)}) async-start(), calls=%async_computation.3 | async-start | bytes 15597568 | tf_op jit(solution)/shard_map/all_gather | solution.py:80
  7.9 371.4 %all-gather.5.cloned.1.call-start = ((), (), s32[]{:S(2)}) async-start(), calls=%async_computation.4 | async-start | bytes 15597568 | tf_op jit(solution)/shard_map/all_gather | solution.py:85
  8.7 32.5 %collective-permute-start = (bf16[1,3584,128]{2,1,0:T(8,128)(2,1)}, bf16[1,3584,128]{2,1,0:T(8,128)(2,1)S(1)}, u32[]{:S(2)}, u32[]{:S(2)}) collective-permute-start(bf16[1,3584,128]{2,1,0:T(8,128)(2,1)} %param.16), channel_id=1, source_target_pairs={{0,8},{8,16},{16,24},{24,32},{32,40},{40,48},{48,56},{56,64},{64,7... | collective-permute-start | bytes 2752520 | tf_op jit(solution)/shard_map/ppermute | solution.py:15
  41.2 31.0 %collective-permute-start.1 = (bf16[1,3584,128]{2,1,0:T(8,128)(2,1)S(1)}, bf16[1,3584,128]{2,1,0:T(8,128)(2,1)}, u32[]{:S(2)}, u32[]{:S(2)}) collective-permute-start(bf16[1,3584,128]{2,1,0:T(8,128)(2,1)S(1)} %collective-permute-done), channel_id=1, source_target_pairs={{0,8},{8,16},{16,24},{24,32},{32,40},{40,48},{48,56},{56,64},{64,7... | collective-permute-start | bytes 2752520 | tf_op jit(solution)/shard_map/ppermute | solution.py:15
  41.2 31.0 %collective-permute-start.8 = (bf16[1,3584,128]{2,1,0:T(8,128)(2,1)}, bf16[1,3584,128]{2,1,0:T(8,128)(2,1)}, u32[]{:S(2)}, u32[]{:S(2)}) collective-permute-start(bf16[1,3584,128]{2,1,0:T(8,128)(2,1)} %param.16), channel_id=1, source_target_pairs={{0,120},{8,0},{16,8},{24,16},{32,24},{40,32},{48,40},{56,48},{64,5... | collective-permute-start | bytes 2752520 | tf_op jit(solution)/shard_map/ppermute | solution.py:17
  72.2 45.1 %collective-permute-start.2 = (bf16[1,3584,128]{2,1,0:T(8,128)(2,1)}, bf16[1,3584,128]{2,1,0:T(8,128)(2,1)S(1)}, u32[]{:S(2)}, u32[]{:S(2)}) collective-permute-start(bf16[1,3584,128]{2,1,0:T(8,128)(2,1)} %collective-permute-done.1), channel_id=1, source_target_pairs={{0,8},{8,16},{16,24},{24,32},{32,40},{40,48},{48,56},{56,64},{64,7... | collective-permute-start | bytes 2752520 | tf_op jit(solution)/shard_map/ppermute | solution.py:15
  72.2 46.0 %collective-permute-start.9 = (bf16[1,3584,128]{2,1,0:T(8,128)(2,1)}, bf16[1,3584,128]{2,1,0:T(8,128)(2,1)}, u32[]{:S(2)}, u32[]{:S(2)}) collective-permute-start(bf16[1,3584,128]{2,1,0:T(8,128)(2,1)} %collective-permute-done.8), channel_id=1, source_target_pairs={{0,120},{8,0},{16,8},{24,16},{32,24},{40,32},{48,40},{56,48},{64,5... | collective-permute-start | bytes 2752520 | tf_op jit(solution)/shard_map/ppermute | solution.py:17
  117.3 0.9 copy-start.3
  118.2 44.6 %collective-permute-start.3 = (bf16[1,3584,128]{2,1,0:T(8,128)(2,1)S(1)}, bf16[1,3584,128]{2,1,0:T(8,128)(2,1)S(1)}, u32[]{:S(2)}, u32[]{:S(2)}) collective-permute-start(bf16[1,3584,128]{2,1,0:T(8,128)(2,1)S(1)} %collective-permute-done.2), channel_id=1, source_target_pairs={{0,8},{8,16},{16,24},{24,32},{32,40},{40,48},{48,56},{56,64},{64,7... | collective-permute-start | bytes 2752520 | tf_op jit(solution)/shard_map/ppermute | solution.py:15
  118.2 44.6 %collective-permute-start.10 = (bf16[1,3584,128]{2,1,0:T(8,128)(2,1)}, bf16[1,3584,128]{2,1,0:T(8,128)(2,1)S(1)}, u32[]{:S(2)}, u32[]{:S(2)}) collective-permute-start(bf16[1,3584,128]{2,1,0:T(8,128)(2,1)} %collective-permute-done.9), channel_id=1, source_target_pairs={{0,120},{8,0},{16,8},{24,16},{32,24},{40,32},{48,40},{56,48},{64,5... | collective-permute-start | bytes 2752520 | tf_op jit(solution)/shard_map/ppermute | solution.py:17
  162.8 1.0 copy-start.7
  162.8 24.3 %collective-permute-start.4 = (bf16[1,3584,128]{2,1,0:T(8,128)(2,1)S(1)}, bf16[1,3584,128]{2,1,0:T(8,128)(2,1)}, u32[]{:S(2)}, u32[]{:S(2)}) collective-permute-start(bf16[1,3584,128]{2,1,0:T(8,128)(2,1)S(1)} %collective-permute-done.3), channel_id=1, source_target_pairs={{0,8},{8,16},{16,24},{24,32},{32,40},{40,48},{48,56},{56,64},{64,7... | collective-permute-start | bytes 2752520 | tf_op jit(solution)/shard_map/ppermute | solution.py:15
  163.7 66.0 %copy-start.5 = (bf16[1,3584,128]{2,1,0:T(8,128)(2,1)}, bf16[1,3584,128]{2,1,0:T(8,128)(2,1)S(1)}, u32[]{:S(2)}) copy-start(bf16[1,3584,128]{2,1,0:T(8,128)(2,1)S(1)} %collective-permute-done.10) | copy-start | bytes 2752516
  163.7 27.0 %collective-permute-start.11 = (bf16[1,3584,128]{2,1,0:T(8,128)(2,1)S(1)}, bf16[1,3584,128]{2,1,0:T(8,128)(2,1)}, u32[]{:S(2)}, u32[]{:S(2)}) collective-permute-start(bf16[1,3584,128]{2,1,0:T(8,128)(2,1)S(1)} %collective-permute-done.10), channel_id=1, source_target_pairs={{0,120},{8,0},{16,8},{24,16},{32,24},{40,32},{48,40},{56,48},{64,5... | collective-permute-start | bytes 2752520 | tf_op jit(solution)/shard_map/ppermute | solution.py:17
  187.1 38.4 %collective-permute-start.5 = (bf16[1,3584,128]{2,1,0:T(8,128)(2,1)}, bf16[1,3584,128]{2,1,0:T(8,128)(2,1)}, u32[]{:S(2)}, u32[]{:S(2)}) collective-permute-start(bf16[1,3584,128]{2,1,0:T(8,128)(2,1)} %collective-permute-done.4), channel_id=1, source_target_pairs={{0,8},{8,16},{16,24},{24,32},{32,40},{40,48},{48,56},{56,64},{64,7... | collective-permute-start | bytes 2752520 | tf_op jit(solution)/shard_map/ppermute | solution.py:15
  190.8 43.5 %collective-permute-start.12 = (bf16[1,3584,128]{2,1,0:T(8,128)(2,1)}, bf16[1,3584,128]{2,1,0:T(8,128)(2,1)}, u32[]{:S(2)}, u32[]{:S(2)}) collective-permute-start(bf16[1,3584,128]{2,1,0:T(8,128)(2,1)} %collective-permute-done.11), channel_id=1, source_target_pairs={{0,120},{8,0},{16,8},{24,16},{32,24},{40,32},{48,40},{56,48},{64,5... | collective-permute-start | bytes 2752520 | tf_op jit(solution)/shard_map/ppermute | solution.py:17
  225.5 37.6 %collective-permute-start.6 = (bf16[1,3584,128]{2,1,0:T(8,128)(2,1)}, bf16[1,3584,128]{2,1,0:T(8,128)(2,1)}, u32[]{:S(2)}, u32[]{:S(2)}) collective-permute-start(bf16[1,3584,128]{2,1,0:T(8,128)(2,1)} %collective-permute-done.5), channel_id=1, source_target_pairs={{0,8},{8,16},{16,24},{24,32},{32,40},{40,48},{48,56},{56,64},{64,7... | collective-permute-start | bytes 2752520 | tf_op jit(solution)/shard_map/ppermute | solution.py:15
  229.8 33.4 %all-to-all-start = ((bf16[4,96,2048]{2,1,0:T(8,128)(2,1)}), bf16[4,96,2048]{2,1,0:T(8,128)(2,1)S(1)}, u32[]{:S(2)}, u32[]{:S(2)}) async-start(bf16[4,96,2048]{2,1,0:T(8,128)(2,1)} %bitcast.2), calls=%async_computation | async-start | bytes 3145728 | tf_op jit(solution)/shard_map/all_to_all | solution.py:71
  234.3 44.7 %collective-permute-start.13 = (bf16[1,3584,128]{2,1,0:T(8,128)(2,1)}, bf16[1,3584,128]{2,1,0:T(8,128)(2,1)}, u32[]{:S(2)}, u32[]{:S(2)}) collective-permute-start(bf16[1,3584,128]{2,1,0:T(8,128)(2,1)} %collective-permute-done.12), channel_id=1, source_target_pairs={{0,120},{8,0},{16,8},{24,16},{32,24},{40,32},{48,40},{56,48},{64,5... | collective-permute-start | bytes 2752520 | tf_op jit(solution)/shard_map/ppermute | solution.py:17
  263.1 42.9 %collective-permute-start.7 = (bf16[1,3584,128]{2,1,0:T(8,128)(2,1)}, bf16[1,3584,128]{2,1,0:T(8,128)(2,1)}, u32[]{:S(2)}, u32[]{:S(2)}) collective-permute-start(bf16[1,3584,128]{2,1,0:T(8,128)(2,1)} %collective-permute-done.6), channel_id=1, source_target_pairs={{0,8},{8,16},{16,24},{24,32},{32,40},{40,48},{48,56},{56,64},{64,7... | collective-permute-start | bytes 2752520 | tf_op jit(solution)/shard_map/ppermute | solution.py:15
  263.1 116.2 %copy-start.1 = (bf16[4,96,2048]{2,1,0:T(8,128)(2,1)}, bf16[4,96,2048]{2,1,0:T(8,128)(2,1)S(1)}, u32[]{:S(2)}) copy-start(bf16[4,96,2048]{2,1,0:T(8,128)(2,1)S(1)} %all-to-all-done) | copy-start | bytes 4718596
  263.1 85.2 %copy-start.8 = (bf16[1,3584,128]{2,1,0:T(8,128)(2,1)S(1)}, bf16[1,3584,128]{2,1,0:T(8,128)(2,1)}, u32[]{:S(2)}) copy-start(bf16[1,3584,128]{2,1,0:T(8,128)(2,1)} %copy-done.7) | copy-start | bytes 2752516
  263.1 86.2 %copy-start.4 = (bf16[1,3584,128]{2,1,0:T(8,128)(2,1)S(1)}, bf16[1,3584,128]{2,1,0:T(8,128)(2,1)}, u32[]{:S(2)}) copy-start(bf16[1,3584,128]{2,1,0:T(8,128)(2,1)} %copy-done.3) | copy-start | bytes 2752516
  263.2 96.2 %copy-start.6 = (bf16[1,3584,128]{2,1,0:T(8,128)(2,1)S(1)}, bf16[1,3584,128]{2,1,0:T(8,128)(2,1)}, u32[]{:S(2)}) copy-start(bf16[1,3584,128]{2,1,0:T(8,128)(2,1)} %copy-done.5) | copy-start | bytes 2752516
  279.0 59.3 %collective-permute-start.14 = (bf16[1,3584,128]{2,1,0:T(8,128)(2,1)}, bf16[1,3584,128]{2,1,0:T(8,128)(2,1)S(1)}, u32[]{:S(2)}, u32[]{:S(2)}) collective-permute-start(bf16[1,3584,128]{2,1,0:T(8,128)(2,1)} %collective-permute-done.13), channel_id=1, source_target_pairs={{0,120},{8,0},{16,8},{24,16},{32,24},{40,32},{48,40},{56,48},{64,5... | collective-permute-start | bytes 2752520 | tf_op jit(solution)/shard_map/ppermute | solution.py:17
  379.3 11.6 %copy-start.12 = (bf16[1,16,3584]{2,1,0:T(8,128)(2,1)S(1)}, bf16[1,16,3584]{2,1,0:T(8,128)(2,1)}, u32[]{:S(2)}) copy-start(bf16[1,16,3584]{2,1,0:T(8,128)(2,1)} %param.18) | copy-start | bytes 344068
  390.8 52.9 %copy-start.9 = (bf16[128,2048]{1,0:T(8,128)(2,1)S(1)}, bf16[128,2048]{1,0:T(8,128)(2,1)}, u32[]{:S(2)}) copy-start(bf16[128,2048]{1,0:T(8,128)(2,1)} %param.10) | copy-start | bytes 1572868
  390.8 52.9 %copy-start.10 = (f32[384,128]{1,0:T(8,128)S(1)}, f32[384,128]{1,0:T(8,128)}, u32[]{:S(2)}) copy-start(f32[384,128]{1,0:T(8,128)} %get-tuple-element.4) | copy-start | bytes 589828
  390.8 54.2 %copy-start.13 = (s32[128]{0:T(128)S(1)}, s32[128]{0:T(128)}, u32[]{:S(2)}) copy-start(s32[128]{0:T(128)} %param.13) | copy-start | bytes 1540
  449.5 23.9 %all-to-all-start.2 = ((bf16[4,96,2048]{2,1,0:T(8,128)(2,1)}), bf16[4,96,2048]{2,1,0:T(8,128)(2,1)S(1)}, u32[]{:S(2)}, u32[]{:S(2)}) async-start(bf16[4,96,2048]{2,1,0:T(8,128)(2,1)} %bitcast.11), calls=%async_computation.2 | async-start | bytes 3145728 | tf_op jit(solution)/shard_map/all_to_all | solution.py:115
  453.0 126.9 %all-reduce.4.cloned.1.call-start = ((), (), s32[]{:S(2)}) async-start(), calls=%async_computation.5 | async-start | bytes 131072 | tf_op jit(solution)/shard_map/psum | solution.py:133
  473.4 1.2 copy-start.11
  488.7 176.9 %all-reduce.6.cloned.1.call-start = ((), (), s32[]{:S(2)}) async-start(), calls=%async_computation.6 | async-start | bytes 229376 | tf_op jit(solution)/shard_map/psum | solution.py:134
Sparse Core Ops, SparseCore 0:
  10.1 161.0 all-gather.2
  173.4 159.5 all-gather.4
  488.8 91.0 all-reduce.3
  583.6 81.9 all-reduce.5
